TPU v7x, 128 devices: a whole 4x4x4 slice. The times are simulated.
128 devices in a mesh: wide: 16 (over y, x), narrow: 8 (over z, core).
Axes of the slice: x: 4, y: 4, z: 4, core: 2. Of those that a mesh axis runs over, the one named last changes fastest.
Arguments:
- tokens: bfloat16 [256, 128, 1536], P('wide'), may hold values from -8 to 8
- ln_gain: bfloat16 [1536], replicated, may hold values from 0.3984375 to 1.59375
- gate_weight: bfloat16 [1536, 8960], P(None, 'narrow'), may hold values from -0.15625 to 0.15625
- up_weight: bfloat16 [1536, 8960], P(None, 'narrow'), may hold values from -0.15625 to 0.15625
- down_weight: bfloat16 [8960, 1536], P('narrow'), may hold values from -0.0625 to 0.0625
- out_gain: bfloat16 [1536], replicated, may hold values from 0.25 to 1.75
- shard_ids: int32 [256], P('wide'), may hold values from 0 to 15, as said below
- slab_old: bfloat16 [262144, 1536], P(('wide', 'narrow')), may hold values from -8 to 8
- queries: bfloat16 [16, 64, 1536], P('wide'), may hold values from -12 to 12
- positives: int32 [16, 64], P('wide'), may hold values from 0 to 262399
- owners: int32 [4], replicated, may hold values from 0 to 15
Outputs:
- index_new: bfloat16 [16, 16, 2, 1536], P('wide', 'narrow')
- losses: float32 [4, 64], replicated
Inputs may be any that keep to these rules, and one draw needn't show every extreme that they name: `shard_ids`: among the 16 passages of one index of wide at most 2 have the same shard id; in every draw one shard id is held by exactly 2 passages of every index of wide.
All inputs are finite; a program needn't handle non-finite values.
Results may differ from a plain program's by a relative error of at most 0.0029.
Values may be sent and summed in bfloat16 or wider, within the bound.
No kernel may reach another device: no remote copies, remote signals or barrier semaphores. Data moves between devices by JAX's collectives and lax.ppermute only.
A program may use at most 128 MiB of HBM per device.

v0:
```python
import math
import jax
import jax.numpy as jnp
from jax import lax
from jax.sharding import PartitionSpec as P

EPS = 1e-06


def spread(x, axis, root):
    mine = lax.axis_index(axis) == root
    return lax.psum(jnp.where(mine, x, jnp.zeros_like(x)), axis)


def rms_scale(values):
    return lax.rsqrt(jnp.mean(values * values, axis=-1, keepdims=True) + EPS)


def local(
    tokens,
    ln_gain,
    gate_weight,
    up_weight,
    down_weight,
    out_gain,
    shard_ids,
    slab_old,
    queries,
    positives,
    owners,
):
    passages, seq_len, width = tokens.shape
    narrow_count = lax.axis_size("narrow")
    wide_count = lax.axis_size("wide")
    narrow_rank = lax.axis_index("narrow")
    wide_rank = lax.axis_index("wide")
    piece_width = width // narrow_count
    capacity = 2 * passages // wide_count
    values = tokens.astype(jnp.float32)
    normed = (values * rms_scale(values) * ln_gain.astype(jnp.float32)).astype(jnp.bfloat16)
    normed = normed.reshape(passages * seq_len, width)
    gate = jnp.dot(normed, gate_weight, preferred_element_type=jnp.float32)
    upward = jnp.dot(normed, up_weight, preferred_element_type=jnp.float32)
    hidden = (jax.nn.silu(gate) * upward).astype(jnp.bfloat16)
    partial_value = jnp.dot(hidden, down_weight, preferred_element_type=jnp.float32)
    pooled_part = jnp.mean(partial_value.reshape(passages, seq_len, width), axis=1)
    token_mean = jnp.mean(values, axis=1)
    offset = narrow_rank * piece_width
    pooled = lax.psum(pooled_part, "narrow") + token_mean
    norm_scale = rms_scale(pooled)
    own_piece = lax.dynamic_slice_in_dim(pooled, offset, piece_width, 1)
    gain_piece = lax.dynamic_slice_in_dim(out_gain.astype(jnp.float32), offset, piece_width, 0)
    embedding = (own_piece * norm_scale * gain_piece).astype(jnp.bfloat16)
    positions = jnp.arange(passages, dtype=jnp.int32)
    earlier = positions[:, None] > positions[None, :]
    same = shard_ids[:, None] == shard_ids[None, :]
    rank = jnp.sum((earlier & same).astype(jnp.int32), axis=1)
    slots = shard_ids * capacity + rank
    dispatch = slots[None, :] == jnp.arange(wide_count * capacity, dtype=jnp.int32)[:, None]
    outgoing = jnp.dot(dispatch.astype(jnp.bfloat16), embedding, preferred_element_type=jnp.float32)
    outgoing = outgoing.astype(jnp.bfloat16).reshape(wide_count, capacity, piece_width)
    numbers = wide_rank * passages + positions
    slot_numbers = jnp.sum(jnp.where(dispatch, numbers[None, :] + 1, 0), axis=1) - 1
    slot_numbers = slot_numbers.reshape(wide_count, capacity, 1)
    arrived, arrived_numbers = (
        lax.all_to_all(
            lax.all_to_all(outgoing, "wide", split_axis=0, concat_axis=0, tiled=True),
            "narrow",
            split_axis=0,
            concat_axis=2,
            tiled=True,
        ),
        lax.all_to_all(
            lax.all_to_all(slot_numbers, "wide", split_axis=0, concat_axis=0, tiled=True),
            "narrow",
            split_axis=0,
            concat_axis=2,
            tiled=True,
        ),
    )
    old_total = slab_old.shape[0] * wide_count * narrow_count
    new_rows = arrived.reshape(-1, width)
    new_numbers = arrived_numbers[:, :, 0].reshape(-1)
    valid = (new_numbers >= 0)[None, :]
    new_global = old_total + new_numbers
    device_linear = wide_rank * narrow_count + narrow_rank
    old_global = device_linear * slab_old.shape[0] + jnp.arange(slab_old.shape[0], dtype=jnp.int32)
    scale = 1.0 / math.sqrt(width)
    contract = (((1,), (1,)), ((), ()))
    block_size = queries.shape[1]
    step_count = owners.shape[0]

    def score_rows(block, positive):
        old_scores = (
            lax.dot_general(block, slab_old, contract, preferred_element_type=jnp.float32) * scale
        )
        new_scores = (
            lax.dot_general(block, new_rows, contract, preferred_element_type=jnp.float32) * scale
        )
        masked = jnp.where(valid, new_scores, -jnp.inf)
        local_max = jnp.maximum(jnp.max(old_scores, axis=1), jnp.max(masked, axis=1))
        hit_old = old_global[None, :] == positive[:, None]
        hit_new = valid & (new_global[None, :] == positive[:, None])
        local_positive = jnp.sum(jnp.where(hit_old, old_scores, 0.0), axis=1) + jnp.sum(
            jnp.where(hit_new, new_scores, 0.0), axis=1
        )
        largest = lax.pmax(local_max, ("wide", "narrow"))
        local_total = jnp.sum(jnp.exp(old_scores - largest[:, None]), axis=1)
        local_total = local_total + jnp.sum(
            jnp.where(valid, jnp.exp(new_scores - largest[:, None]), 0.0), axis=1
        )
        total, picked = lax.psum((local_total, local_positive), ("wide", "narrow"))
        return largest + jnp.log(total) - picked

    def step_body(step, losses):
        owner = owners[step]
        block, positive = (spread(queries[0], "wide", owner), spread(positives[0], "wide", owner))
        loss = score_rows(block, positive)
        return lax.dynamic_update_slice_in_dim(losses, loss[None, :], step, 0)

    start_losses = jnp.zeros((step_count, block_size), jnp.float32)
    losses = lax.fori_loop(0, step_count, step_body, start_losses)
    return (arrived[None], losses)


def solution(mesh):
    return jax.shard_map(
        local,
        mesh=mesh,
        in_specs=(
            P("wide", None, None),
            P(),
            P(None, "narrow"),
            P(None, "narrow"),
            P("narrow", None),
            P(),
            P("wide"),
            P(("wide", "narrow"), None),
            P("wide", None, None),
            P("wide", None),
            P(),
        ),
        out_specs=(P("wide", "narrow", None, None), P()),
        check_vma=False,
    )
```

profile of v0, /device:TPU:1, one launch (start us, length us, event | category | flops | bytes accessed | tf_op | source)
XLA Modules:
  0.0 1026.5 jit_solution(8330299875181176620)
XLA Ops:
  17.2 9.7 fusion.16
  26.9 22.3 %bitcast_reduce_fusion = f32[16,1536]{1,0:T(8,128)} fusion(bf16[1120,1536]{1,0:T(8,128)(2,1)} %param.17, bf16[2048,1536]{1,0:T(8,128)(2,1)} %bitcast.51, bf16[1536,1120]{0,1:T(8,128)(2,1)} %param.16, f32[2048,1120]{0,1:T(8,128)} %fusion.16), kind=kOutput, calls=%fused_computation.19 | convolution fusion | flops 14109745152 | bytes 22446080 | tf_op jit(solution)/shard_map/dot_general | solution.py:45
  51.8 7.6 all-to-all-start.2
  65.7 7.6 all-to-all-start.3
  78.1 32.4 %all-reduce.6.cloned.1.call-done = f32[16,1536]{1,0:T(8,128)} async-done(((f32[16,1536]{1,0:T(8,128)}), f32[16,1536]{1,0:T(8,128)}) %all-reduce.6.cloned.1.call-update) | async-done | bytes 98320 | tf_op jit(solution)/shard_map/psum | solution.py:49
  113.1 6.6 all-to-all-start
  126.2 7.2 all-to-all-start.1
  138.8 881.1 %while.14 = (s32[]{:T(128)}, f32[4,64]{1,0:T(4,128)}, s32[4]{0:T(128)}, bf16[1,64,1536]{2,1,0:T(8,128)(2,1)}, bf16[2048,1536]{1,0:T(8,128)(2,1)}, /*index=5*/pre...) while((s32[]{:T(128)}, f32[4,64]{1,0:T(4,128)}, ...), condition=%wide.region_19.20_spmd.clone, body=%wide.region_7.19_spmd.clone.sunk | while | flops 404558592 | bytes 10132520 | solution.py:122
  141.6 9.3 psum.59
  150.9 69.7 %all-reduce.8.cloned.1.call-done = bf16[64,1536]{1,0:T(8,128)(2,1)} async-done(((bf16[64,1536]{1,0:T(8,128)(2,1)}), bf16[64,1536]{1,0:T(8,128)(2,1)}) %all-reduce.8.cloned.1.call-update) | async-done | bytes 196624 | tf_op jit(solution)/shard_map/while/body/eval_jaxpr/psum | solution.py:12
  226.6 66.3 %pmax.13 = f32[64]{0:T(128)S(1)} all-reduce(f32[64]{0:T(128)S(1)} %max.11), channel_id=1, replica_groups=mesh['wide'=16,'narrow'=8] {'wide','narrow'}, use_global_device_ids=true, to_apply=%region_11.11 | all-reduce | flops 64 | bytes 512 | tf_op jit(solution)/shard_map/while/body/eval_jaxpr/pmax | solution.py:107
  294.4 62.5 %all-reduce.2 = (f32[64]{0:T(128)S(1)}, f32[64]{0:T(128)S(1)}) all-reduce(f32[64]{0:T(128)S(1)} %add.187, f32[64]{0:T(128)S(1)} %add.188), channel_id=1, replica_groups=mesh['wide'=16,'narrow'=8] {'wide','narrow'}, use_global_device_ids=true, to_apply=%region_18.18 | all-reduce | flops 128 | bytes 1024 | tf_op jit(solution)/shard_map/while/body/eval_jaxpr/psum | solution.py:112
  361.0 10.9 %psum.59 = s32[64]{0:T(128)S(1)} all-reduce(s32[64]{0:T(128)S(1)} %fusion.37), channel_id=1, replica_groups=mesh['wide'=16,'narrow'=8] {'wide'}, use_global_device_ids=true, to_apply=%region_15.15 | all-reduce | flops 64 | bytes 512 | tf_op jit(solution)/shard_map/while/body/eval_jaxpr/psum | solution.py:12
  371.8 69.6 %all-reduce.8.cloned.1.call-done = bf16[64,1536]{1,0:T(8,128)(2,1)} async-done(((bf16[64,1536]{1,0:T(8,128)(2,1)}), bf16[64,1536]{1,0:T(8,128)(2,1)}) %all-reduce.8.cloned.1.call-update) | async-done | bytes 196624 | tf_op jit(solution)/shard_map/while/body/eval_jaxpr/psum | solution.py:12
  447.4 66.4 %pmax.13 = f32[64]{0:T(128)S(1)} all-reduce(f32[64]{0:T(128)S(1)} %max.11), channel_id=1, replica_groups=mesh['wide'=16,'narrow'=8] {'wide','narrow'}, use_global_device_ids=true, to_apply=%region_11.11 | all-reduce | flops 64 | bytes 512 | tf_op jit(solution)/shard_map/while/body/eval_jaxpr/pmax | solution.py:107
  515.2 62.5 %all-reduce.2 = (f32[64]{0:T(128)S(1)}, f32[64]{0:T(128)S(1)}) all-reduce(f32[64]{0:T(128)S(1)} %add.187, f32[64]{0:T(128)S(1)} %add.188), channel_id=1, replica_groups=mesh['wide'=16,'narrow'=8] {'wide','narrow'}, use_global_device_ids=true, to_apply=%region_18.18 | all-reduce | flops 128 | bytes 1024 | tf_op jit(solution)/shard_map/while/body/eval_jaxpr/psum | solution.py:112
  583.3 9.0 psum.59
  592.3 69.5 %all-reduce.8.cloned.1.call-done = bf16[64,1536]{1,0:T(8,128)(2,1)} async-done(((bf16[64,1536]{1,0:T(8,128)(2,1)}), bf16[64,1536]{1,0:T(8,128)(2,1)}) %all-reduce.8.cloned.1.call-update) | async-done | bytes 196624 | tf_op jit(solution)/shard_map/while/body/eval_jaxpr/psum | solution.py:12
  667.9 66.3 %pmax.13 = f32[64]{0:T(128)S(1)} all-reduce(f32[64]{0:T(128)S(1)} %max.11), channel_id=1, replica_groups=mesh['wide'=16,'narrow'=8] {'wide','narrow'}, use_global_device_ids=true, to_apply=%region_11.11 | all-reduce | flops 64 | bytes 512 | tf_op jit(solution)/shard_map/while/body/eval_jaxpr/pmax | solution.py:107
  735.7 62.5 %all-reduce.2 = (f32[64]{0:T(128)S(1)}, f32[64]{0:T(128)S(1)}) all-reduce(f32[64]{0:T(128)S(1)} %add.187, f32[64]{0:T(128)S(1)} %add.188), channel_id=1, replica_groups=mesh['wide'=16,'narrow'=8] {'wide','narrow'}, use_global_device_ids=true, to_apply=%region_18.18 | all-reduce | flops 128 | bytes 1024 | tf_op jit(solution)/shard_map/while/body/eval_jaxpr/psum | solution.py:112
  802.2 11.2 %psum.59 = s32[64]{0:T(128)S(1)} all-reduce(s32[64]{0:T(128)S(1)} %fusion.37), channel_id=1, replica_groups=mesh['wide'=16,'narrow'=8] {'wide'}, use_global_device_ids=true, to_apply=%region_15.15 | all-reduce | flops 64 | bytes 512 | tf_op jit(solution)/shard_map/while/body/eval_jaxpr/psum | solution.py:12
  813.4 68.9 %all-reduce.8.cloned.1.call-done = bf16[64,1536]{1,0:T(8,128)(2,1)} async-done(((bf16[64,1536]{1,0:T(8,128)(2,1)}), bf16[64,1536]{1,0:T(8,128)(2,1)}) %all-reduce.8.cloned.1.call-update) | async-done | bytes 196624 | tf_op jit(solution)/shard_map/while/body/eval_jaxpr/psum | solution.py:12
  888.4 66.3 %pmax.13 = f32[64]{0:T(128)S(1)} all-reduce(f32[64]{0:T(128)S(1)} %max.11), channel_id=1, replica_groups=mesh['wide'=16,'narrow'=8] {'wide','narrow'}, use_global_device_ids=true, to_apply=%region_11.11 | all-reduce | flops 64 | bytes 512 | tf_op jit(solution)/shard_map/while/body/eval_jaxpr/pmax | solution.py:107
  956.2 62.5 %all-reduce.2 = (f32[64]{0:T(128)S(1)}, f32[64]{0:T(128)S(1)}) all-reduce(f32[64]{0:T(128)S(1)} %add.187, f32[64]{0:T(128)S(1)} %add.188), channel_id=1, replica_groups=mesh['wide'=16,'narrow'=8] {'wide','narrow'}, use_global_device_ids=true, to_apply=%region_18.18 | all-reduce | flops 128 | bytes 1024 | tf_op jit(solution)/shard_map/while/body/eval_jaxpr/psum | solution.py:112
  (110 shorter events, 82.9 us)
Async XLA Ops:
  7.2 10.1 copy-start
  7.2 103.3 %all-reduce.6.cloned.1.call-start = ((), (), s32[]{:S(2)}) async-start(), calls=%async_computation.4 | async-start | bytes 196608 | tf_op jit(solution)/shard_map/psum | solution.py:49
  7.2 5.8 copy-start.1
  14.5 2.7 copy-start.2
  26.9 23.8 %copy-start.4 = (s32[16]{0:T(128)S(1)}, s32[16]{0:T(128)}, u32[]{:S(2)}) copy-start(s32[16]{0:T(128)} %param.19) | copy-start | bytes 196
  50.9 26.9 %copy-start.5 = (s32[16]{0:T(128)}, s32[16]{0:T(128)S(1)}, u32[]{:S(2)}) copy-start(s32[16]{0:T(128)S(1)} %multiply_add_fusion.1) | copy-start | bytes 196
  51.8 13.9 %all-to-all-start.2 = ((s32[16,2,1]{1,2,0:T(1,128)}), s32[16,2,1]{1,2,0:T(1,128)}, u32[]{:S(2)}, u32[]{:S(2)}) async-start(s32[16,2,1]{1,2,0:T(1,128)} %bitcast.4), calls=%async_computation.2 | async-start | bytes 16384 | tf_op jit(solution)/shard_map/all_to_all | solution.py:74
  65.7 12.2 %all-to-all-start.3 = ((s32[16,2,1]{1,2,0:T(1,128)}), s32[16,2,1]{1,2,0:T(1,128)S(1)}, u32[]{:S(2)}, u32[]{:S(2)}) async-start(s32[16,2,1]{1,2,0:T(1,128)} %all-to-all-done.2), calls=%async_computation.3 | async-start | bytes 16384 | tf_op jit(solution)/shard_map/all_to_all | solution.py:73
  113.1 13.1 %all-to-all-start = ((bf16[16,2,192]{2,1,0:T(2,128)(2,1)}), bf16[16,2,192]{2,1,0:T(2,128)(2,1)}, u32[]{:S(2)}, u32[]{:S(2)}) async-start(bf16[16,2,192]{2,1,0:T(2,128)(2,1)} %reshape.84), calls=%async_computation | async-start | bytes 32768 | tf_op jit(solution)/shard_map/all_to_all | solution.py:67
  126.2 11.9 %all-to-all-start.1 = ((bf16[16,2,192]{2,1,0:T(2,128)(2,1)}), bf16[16,2,192]{2,1,0:T(2,128)(2,1)S(1)}, u32[]{:S(2)}, u32[]{:S(2)}) async-start(bf16[16,2,192]{2,1,0:T(2,128)(2,1)} %all-to-all-done), calls=%async_computation.1 | async-start | bytes 32768 | tf_op jit(solution)/shard_map/all_to_all | solution.py:66
  138.8 81.8 %all-reduce.8.cloned.1.call-start = ((), (), s32[]{:S(2)}) async-start(), calls=%async_computation.5 | async-start | bytes 393216 | tf_op jit(solution)/shard_map/while/body/eval_jaxpr/psum | solution.py:12
  220.6 5.8 copy-start.3
  358.2 83.2 %all-reduce.8.cloned.1.call-start = ((), (), s32[]{:S(2)}) async-start(), calls=%async_computation.5 | async-start | bytes 393216 | tf_op jit(solution)/shard_map/while/body/eval_jaxpr/psum | solution.py:12
  441.4 5.8 copy-start.3
  579.0 82.9 %all-reduce.8.cloned.1.call-start = ((), (), s32[]{:S(2)}) async-start(), calls=%async_computation.5 | async-start | bytes 393216 | tf_op jit(solution)/shard_map/while/body/eval_jaxpr/psum | solution.py:12
  661.9 5.8 copy-start.3
  799.5 82.9 %all-reduce.8.cloned.1.call-start = ((), (), s32[]{:S(2)}) async-start(), calls=%async_computation.5 | async-start | bytes 393216 | tf_op jit(solution)/shard_map/while/body/eval_jaxpr/psum | solution.py:12
  882.4 5.8 copy-start.3
Sparse Core Ops, SparseCore 0:
  50.9 59.5 all-reduce.5
  142.8 77.7 all-reduce.7
  362.2 79.1 all-reduce.7
  582.8 79.0 all-reduce.7
  803.2 79.1 all-reduce.7
where the time goes:
time: 1030 us
  blocking collectives  556 us (54%)
  waiting for transfers between devices  330 us (32%)
  matrix products  56.9 us (6%)
  starting transfers between devices  29 us (3%)
  other arithmetic  22 us (2%)
  local copies, waits for them, and re-layouts  15.6 us (2%)
  between operations  13.8 us (1%)
    psum x4, waiting for transfers between devices, spread(): return lax.psum(jnp.where(mine, x, jnp.zeros_like(x)), axis)  278 us
    pmax x4, blocking collectives, score_rows(): largest = lax.pmax(local_max, ('wide', 'narrow'))  265 us
    psum x4, blocking collectives, score_rows(): total, picked = lax.psum((local_total, local_positive), ('wide', 'narrow'))  250 us
    psum x4, blocking collectives, spread(): return lax.psum(jnp.where(mine, x, jnp.zeros_like(x)), axis)  40.4 us
    psum x1, waiting for transfers between devices, local(): pooled = lax.psum(pooled_part, 'narrow') + token_mean  32.4 us
    dot_general x4, matrix products, score_rows(): lax.dot_general(block, slab_old, contract, preferred_element_type=jnp.flo...  23.3 us
    dot_general x1, matrix products, local(): jnp.dot(hidden, down_weight, preferred_element_type=jnp.float32)  22.3 us
  transfers between devices with their start and end apart: 9, of which 9 were waited for; matrix products, arithmetic and copies ran while one was open for 0% of the time, Pallas kernels for 0%

commit v1 on v0

--- a/solution.py
+++ b/solution.py
@@ -109,7 +109,13 @@
         local_total = local_total + jnp.sum(
             jnp.where(valid, jnp.exp(new_scores - largest[:, None]), 0.0), axis=1
         )
-        total, picked = lax.psum((local_total, local_positive), ("wide", "narrow"))
+
+        def point_tiles(mesh_dim, along_axis, target):
+            for num in (along_axis, mesh_dim):
+                target = lax.psum(target, num)
+            return target
+
+        total, picked = point_tiles("wide", "narrow", (local_total, local_positive))
         return largest + jnp.log(total) - picked
 
     def step_body(step, losses):

time: 1030 us -> 968 us (0.940)
  blocking collectives: 556 us -> 470 us
  waiting for transfers between devices: 330 us -> 350 us
    psum x4 -> x8, blocking collectives: 250 us -> 174 us  [point_tiles(): target = lax.psum(target, num)]
    psum x4, waiting for transfers between devices: 278 us -> 297 us  [spread(): return lax.psum(jnp.where(mine, x, jnp.zeros_like(x)), axis)]
where the time goes in v1:
time: 968 us; the launch traced here: 960 us
  blocking collectives  470 us (49%)
  waiting for transfers between devices  350 us (36%)
  matrix products  56.9 us (6%)
  starting transfers between devices  29 us (3%)
  other arithmetic  22 us (2%)
  local copies, waits for them, and re-layouts  15.6 us (2%)
  between operations  13.8 us (1%)
    psum x4, waiting for transfers between devices, spread(): return lax.psum(jnp.where(mine, x, jnp.zeros_like(x)), axis)  297 us
    pmax x4, blocking collectives, score_rows(): largest = lax.pmax(local_max, ('wide', 'narrow'))  265 us
    psum x8, blocking collectives, point_tiles(): target = lax.psum(target, num)  174 us
    psum x1, waiting for transfers between devices, local(): pooled = lax.psum(pooled_part, 'narrow') + token_mean  32.4 us
    psum x4, blocking collectives, spread(): return lax.psum(jnp.where(mine, x, jnp.zeros_like(x)), axis)  30.6 us
    dot_general x4, matrix products, score_rows(): lax.dot_general(block, slab_old, contract, preferred_element_type=jnp.flo...  23.3 us
    dot_general x1, matrix products, local(): jnp.dot(hidden, down_weight, preferred_element_type=jnp.float32)  22.3 us
  transfers between devices with their start and end apart: 9, of which 9 were waited for; matrix products, arithmetic and copies ran while one was open for 0% of the time, Pallas kernels for 0%

profile of v1, /device:TPU:1, one launch (start us, length us, event | category | flops | bytes accessed | tf_op | source)
XLA Modules:
  0.0 960.3 jit_solution(8154722622802800495)
XLA Ops:
  17.2 9.7 %fusion.16 = f32[2048,1120]{0,1:T(8,128)} fusion(bf16[2048,1536]{1,0:T(8,128)(2,1)S(1)} %bitcast.50, bf16[1536,1120]{0,1:T(8,128)(2,1)S(1)} %copy-done), kind=kOutput, calls=%fused_computation.49 | convolution fusion | flops 7046430720 | bytes 18907136 | tf_op jit(solution)/shard_map/dot_general | solution.py:42
  26.9 22.3 %bitcast_reduce_fusion = f32[16,1536]{1,0:T(8,128)} fusion(bf16[1120,1536]{1,0:T(8,128)(2,1)} %param.17, bf16[2048,1536]{1,0:T(8,128)(2,1)} %bitcast.51, bf16[1536,1120]{0,1:T(8,128)(2,1)} %param.16, f32[2048,1120]{0,1:T(8,128)} %fusion.16), kind=kOutput, calls=%fused_computation.19 | convolution fusion | flops 14109745152 | bytes 22446080 | tf_op jit(solution)/shard_map/dot_general | solution.py:45
  51.8 7.6 all-to-all-start.2
  65.7 7.6 all-to-all-start.3
  78.1 32.4 %all-reduce.9.cloned.1.call-done = f32[16,1536]{1,0:T(8,128)} async-done(((f32[16,1536]{1,0:T(8,128)}), f32[16,1536]{1,0:T(8,128)}) %all-reduce.9.cloned.1.call-update) | async-done | bytes 98320 | tf_op jit(solution)/shard_map/psum | solution.py:49
  138.8 814.9 %while.14 = (s32[]{:T(128)}, f32[4,64]{1,0:T(4,128)}, s32[4]{0:T(128)}, bf16[1,64,1536]{2,1,0:T(8,128)(2,1)}, bf16[2048,1536]{1,0:T(8,128)(2,1)}, /*index=5*/pre...) while((s32[]{:T(128)}, f32[4,64]{1,0:T(4,128)}, ...), condition=%wide.region_21.22_spmd.clone, body=%wide.region_7.21_spmd.clone.sunk | while | flops 404558720 | bytes 10133544 | solution.py:128
  141.6 9.3 psum.83
  150.9 69.7 %all-reduce.11.cloned.1.call-done = bf16[64,1536]{1,0:T(8,128)(2,1)} async-done(((bf16[64,1536]{1,0:T(8,128)(2,1)}), bf16[64,1536]{1,0:T(8,128)(2,1)}) %all-reduce.11.cloned.1.call-update) | async-done | bytes 196624 | tf_op jit(solution)/shard_map/while/body/eval_jaxpr/psum | solution.py:12
  226.6 66.3 %pmax.13 = f32[64]{0:T(128)S(1)} all-reduce(f32[64]{0:T(128)S(1)} %max.11), channel_id=1, replica_groups=mesh['wide'=16,'narrow'=8] {'wide','narrow'}, use_global_device_ids=true, to_apply=%region_11.11 | all-reduce | flops 64 | bytes 512 | tf_op jit(solution)/shard_map/while/body/eval_jaxpr/pmax | solution.py:107
  294.4 12.9 %all-reduce.4 = (f32[64]{0:T(128)S(1)}, f32[64]{0:T(128)S(1)}) all-reduce(f32[64]{0:T(128)S(1)} %add.191, f32[64]{0:T(128)S(1)} %add.192), channel_id=1, replica_groups=mesh['wide'=16,'narrow'=8] {'narrow'}, use_global_device_ids=true, to_apply=%region_19.19 | all-reduce | flops 128 | bytes 1024 | tf_op jit(solution)/shard_map/while/body/eval_jaxpr/psum | solution.py:115
  307.3 30.6 %all-reduce.5 = (f32[64]{0:T(128)S(1)}, f32[64]{0:T(128)S(1)}) all-reduce(f32[64]{0:T(128)S(1)} %get-tuple-element.312, f32[64]{0:T(128)S(1)} %get-tuple-element.313), channel_id=1, replica_groups=mesh['wide'=16,'narrow'=8] {'wide'}, use_global_device_ids=true, to_apply=%region_20.20 | all-reduce | flops 128 | bytes 1024 | tf_op jit(solution)/shard_map/while/body/eval_jaxpr/psum | solution.py:115
  349.1 76.5 %all-reduce.11.cloned.1.call-done = bf16[64,1536]{1,0:T(8,128)(2,1)} async-done(((bf16[64,1536]{1,0:T(8,128)(2,1)}), bf16[64,1536]{1,0:T(8,128)(2,1)}) %all-reduce.11.cloned.1.call-update) | async-done | bytes 196624 | tf_op jit(solution)/shard_map/while/body/eval_jaxpr/psum | solution.py:12
  431.6 66.3 %pmax.13 = f32[64]{0:T(128)S(1)} all-reduce(f32[64]{0:T(128)S(1)} %max.11), channel_id=1, replica_groups=mesh['wide'=16,'narrow'=8] {'wide','narrow'}, use_global_device_ids=true, to_apply=%region_11.11 | all-reduce | flops 64 | bytes 512 | tf_op jit(solution)/shard_map/while/body/eval_jaxpr/pmax | solution.py:107
  499.4 12.9 %all-reduce.4 = (f32[64]{0:T(128)S(1)}, f32[64]{0:T(128)S(1)}) all-reduce(f32[64]{0:T(128)S(1)} %add.191, f32[64]{0:T(128)S(1)} %add.192), channel_id=1, replica_groups=mesh['wide'=16,'narrow'=8] {'narrow'}, use_global_device_ids=true, to_apply=%region_19.19 | all-reduce | flops 128 | bytes 1024 | tf_op jit(solution)/shard_map/while/body/eval_jaxpr/psum | solution.py:115
  512.3 30.6 %all-reduce.5 = (f32[64]{0:T(128)S(1)}, f32[64]{0:T(128)S(1)}) all-reduce(f32[64]{0:T(128)S(1)} %get-tuple-element.312, f32[64]{0:T(128)S(1)} %get-tuple-element.313), channel_id=1, replica_groups=mesh['wide'=16,'narrow'=8] {'wide'}, use_global_device_ids=true, to_apply=%region_20.20 | all-reduce | flops 128 | bytes 1024 | tf_op jit(solution)/shard_map/while/body/eval_jaxpr/psum | solution.py:115
  554.1 76.4 %all-reduce.11.cloned.1.call-done = bf16[64,1536]{1,0:T(8,128)(2,1)} async-done(((bf16[64,1536]{1,0:T(8,128)(2,1)}), bf16[64,1536]{1,0:T(8,128)(2,1)}) %all-reduce.11.cloned.1.call-update) | async-done | bytes 196624 | tf_op jit(solution)/shard_map/while/body/eval_jaxpr/psum | solution.py:12
  636.5 66.3 %pmax.13 = f32[64]{0:T(128)S(1)} all-reduce(f32[64]{0:T(128)S(1)} %max.11), channel_id=1, replica_groups=mesh['wide'=16,'narrow'=8] {'wide','narrow'}, use_global_device_ids=true, to_apply=%region_11.11 | all-reduce | flops 64 | bytes 512 | tf_op jit(solution)/shard_map/while/body/eval_jaxpr/pmax | solution.py:107
  704.3 12.9 %all-reduce.4 = (f32[64]{0:T(128)S(1)}, f32[64]{0:T(128)S(1)}) all-reduce(f32[64]{0:T(128)S(1)} %add.191, f32[64]{0:T(128)S(1)} %add.192), channel_id=1, replica_groups=mesh['wide'=16,'narrow'=8] {'narrow'}, use_global_device_ids=true, to_apply=%region_19.19 | all-reduce | flops 128 | bytes 1024 | tf_op jit(solution)/shard_map/while/body/eval_jaxpr/psum | solution.py:115
  717.1 30.6 %all-reduce.5 = (f32[64]{0:T(128)S(1)}, f32[64]{0:T(128)S(1)}) all-reduce(f32[64]{0:T(128)S(1)} %get-tuple-element.312, f32[64]{0:T(128)S(1)} %get-tuple-element.313), channel_id=1, replica_groups=mesh['wide'=16,'narrow'=8] {'wide'}, use_global_device_ids=true, to_apply=%region_20.20 | all-reduce | flops 128 | bytes 1024 | tf_op jit(solution)/shard_map/while/body/eval_jaxpr/psum | solution.py:115
  751.8 8.7 psum.83
  760.5 74.7 %all-reduce.11.cloned.1.call-done = bf16[64,1536]{1,0:T(8,128)(2,1)} async-done(((bf16[64,1536]{1,0:T(8,128)(2,1)}), bf16[64,1536]{1,0:T(8,128)(2,1)}) %all-reduce.11.cloned.1.call-update) | async-done | bytes 196624 | tf_op jit(solution)/shard_map/while/body/eval_jaxpr/psum | solution.py:12
  841.1 66.3 %pmax.13 = f32[64]{0:T(128)S(1)} all-reduce(f32[64]{0:T(128)S(1)} %max.11), channel_id=1, replica_groups=mesh['wide'=16,'narrow'=8] {'wide','narrow'}, use_global_device_ids=true, to_apply=%region_11.11 | all-reduce | flops 64 | bytes 512 | tf_op jit(solution)/shard_map/while/body/eval_jaxpr/pmax | solution.py:107
  908.9 12.9 %all-reduce.4 = (f32[64]{0:T(128)S(1)}, f32[64]{0:T(128)S(1)}) all-reduce(f32[64]{0:T(128)S(1)} %add.191, f32[64]{0:T(128)S(1)} %add.192), channel_id=1, replica_groups=mesh['wide'=16,'narrow'=8] {'narrow'}, use_global_device_ids=true, to_apply=%region_19.19 | all-reduce | flops 128 | bytes 1024 | tf_op jit(solution)/shard_map/while/body/eval_jaxpr/psum | solution.py:115
  921.8 30.6 %all-reduce.5 = (f32[64]{0:T(128)S(1)}, f32[64]{0:T(128)S(1)}) all-reduce(f32[64]{0:T(128)S(1)} %get-tuple-element.312, f32[64]{0:T(128)S(1)} %get-tuple-element.313), channel_id=1, replica_groups=mesh['wide'=16,'narrow'=8] {'wide'}, use_global_device_ids=true, to_apply=%region_20.20 | all-reduce | flops 128 | bytes 1024 | tf_op jit(solution)/shard_map/while/body/eval_jaxpr/psum | solution.py:115
  (114 shorter events, 109.3 us)
Async XLA Ops:
  7.2 10.1 %copy-start = (bf16[1536,1120]{0,1:T(8,128)(2,1)S(1)}, bf16[1536,1120]{0,1:T(8,128)(2,1)}, u32[]{:S(2)}) copy-start(bf16[1536,1120]{0,1:T(8,128)(2,1)} %param.15) | copy-start | bytes 10321924
  7.2 103.3 %all-reduce.9.cloned.1.call-start = ((), (), s32[]{:S(2)}) async-start(), calls=%async_computation.4 | async-start | bytes 196608 | tf_op jit(solution)/shard_map/psum | solution.py:49
  7.2 5.8 copy-start.1
  14.5 2.7 copy-start.2
  26.9 23.8 %copy-start.4 = (s32[16]{0:T(128)S(1)}, s32[16]{0:T(128)}, u32[]{:S(2)}) copy-start(s32[16]{0:T(128)} %param.19) | copy-start | bytes 196
  50.9 26.9 %copy-start.5 = (s32[16]{0:T(128)}, s32[16]{0:T(128)S(1)}, u32[]{:S(2)}) copy-start(s32[16]{0:T(128)S(1)} %multiply_add_fusion.1) | copy-start | bytes 196
  51.8 13.9 %all-to-all-start.2 = ((s32[16,2,1]{1,2,0:T(1,128)}), s32[16,2,1]{1,2,0:T(1,128)}, u32[]{:S(2)}, u32[]{:S(2)}) async-start(s32[16,2,1]{1,2,0:T(1,128)} %bitcast.4), calls=%async_computation.2 | async-start | bytes 16384 | tf_op jit(solution)/shard_map/all_to_all | solution.py:74
  65.7 12.2 %all-to-all-start.3 = ((s32[16,2,1]{1,2,0:T(1,128)}), s32[16,2,1]{1,2,0:T(1,128)S(1)}, u32[]{:S(2)}, u32[]{:S(2)}) async-start(s32[16,2,1]{1,2,0:T(1,128)} %all-to-all-done.2), calls=%async_computation.3 | async-start | bytes 16384 | tf_op jit(solution)/shard_map/all_to_all | solution.py:73
  113.1 13.1 %all-to-all-start = ((bf16[16,2,192]{2,1,0:T(2,128)(2,1)}), bf16[16,2,192]{2,1,0:T(2,128)(2,1)}, u32[]{:S(2)}, u32[]{:S(2)}) async-start(bf16[16,2,192]{2,1,0:T(2,128)(2,1)} %reshape.84), calls=%async_computation | async-start | bytes 32768 | tf_op jit(solution)/shard_map/all_to_all | solution.py:67
  126.2 11.9 %all-to-all-start.1 = ((bf16[16,2,192]{2,1,0:T(2,128)(2,1)}), bf16[16,2,192]{2,1,0:T(2,128)(2,1)S(1)}, u32[]{:S(2)}, u32[]{:S(2)}) async-start(bf16[16,2,192]{2,1,0:T(2,128)(2,1)} %all-to-all-done), calls=%async_computation.1 | async-start | bytes 32768 | tf_op jit(solution)/shard_map/all_to_all | solution.py:66
  138.8 81.8 %all-reduce.11.cloned.1.call-start = ((), (), s32[]{:S(2)}) async-start(), calls=%async_computation.5 | async-start | bytes 393216 | tf_op jit(solution)/shard_map/while/body/eval_jaxpr/psum | solution.py:12
  220.6 5.8 copy-start.3
  339.2 86.4 %all-reduce.11.cloned.1.call-start = ((), (), s32[]{:S(2)}) async-start(), calls=%async_computation.5 | async-start | bytes 393216 | tf_op jit(solution)/shard_map/while/body/eval_jaxpr/psum | solution.py:12
  425.6 5.8 copy-start.3
  544.2 86.2 %all-reduce.11.cloned.1.call-start = ((), (), s32[]{:S(2)}) async-start(), calls=%async_computation.5 | async-start | bytes 393216 | tf_op jit(solution)/shard_map/while/body/eval_jaxpr/psum | solution.py:12
  630.4 5.8 copy-start.3
  749.0 86.1 %all-reduce.11.cloned.1.call-start = ((), (), s32[]{:S(2)}) async-start(), calls=%async_computation.5 | async-start | bytes 393216 | tf_op jit(solution)/shard_map/while/body/eval_jaxpr/psum | solution.py:12
  835.1 5.8 copy-start.3
Sparse Core Ops, SparseCore 0:
  50.9 59.5 all-reduce.8
  142.8 77.7 all-reduce.10
  343.2 82.3 all-reduce.10
  548.0 82.4 all-reduce.10
  752.7 82.3 all-reduce.10
